TPU v7x, 256 devices: a whole 4x4x8 slice. The times are simulated.
256 devices in a mesh: gx: 64 (over z, x, core), gy: 4 (over y).
Axes of the slice: x: 4, y: 4, z: 8, core: 2. Of those that a mesh axis runs over, the one named last changes fastest.
Arguments:
- pressure: float32 [512, 512, 128], P('gx', 'gy'), may hold values from -6 to 8
- vel_y: float32 [512, 512, 128], P('gx', 'gy'), may hold values from -6 to 6
- vel_z: float32 [512, 512, 128], P('gx', 'gy'), may hold values from -6 to 6
- material: int32 [512, 512, 128], P('gx', 'gy'), may hold values from 0 to 7
- absorb_table: float32 [8], replicated, may hold values from 0.02 to 4
Outputs:
- pressure_next: float32 [512, 512, 128], P('gx', 'gy')
- vel_y_next: float32 [512, 512, 128], P('gx', 'gy')
- vel_z_next: float32 [512, 512, 128], P('gx', 'gy')
All inputs are finite; a program needn't handle non-finite values.
Results may differ from a plain program's by a relative error of at most 0.0004.
Values sent between devices are 32-bit elements; how exact they have to be, the bound alone decides.
A program may use at most 128 MiB of HBM per device.

v0:
```python
import jax
import jax.numpy as jnp
from jax import lax
from jax.sharding import PartitionSpec as P

MATS = 8


def passed_along(value, axis, steps):
    count = lax.axis_size(axis)
    first, last = (max(0, -steps), min(count, count - steps))
    return lax.ppermute(value, axis, [(source, source + steps) for source in range(first, last)])


def join_segments(left, right):
    denom = 1.0 - left[5] * right[1]
    inner_const = (left[3] + left[5] * right[0]) / denom
    inner_left = left[4] / denom
    inner_right = left[5] * right[2] / denom
    outer_const = right[0] + right[1] * inner_const
    outer_left = right[1] * inner_left
    outer_right = right[2] + right[1] * inner_right
    return (
        left[0] + left[2] * outer_const,
        left[1] + left[2] * outer_left,
        left[2] * outer_right,
        right[3] + right[4] * inner_const,
        right[4] * inner_left,
        right[5] + right[4] * inner_right,
    )


def sweep_lines(excess, stacked):

    def forward(carry, items):
        carried, value_prev = carry
        excess_row, value_row = items
        inverse = 1.0 / (1.0 + excess_row + carried)
        value = (value_row + value_prev) * inverse[None]
        carried_next = (excess_row + carried) * inverse
        return ((carried_next, value), (inverse, value))

    start = (jnp.ones(excess.shape[1:], jnp.float32), jnp.zeros(stacked.shape[1:], jnp.float32))
    _, (inverses, values) = lax.scan(forward, start, (excess, stacked))

    def backward(following, items):
        inverse, value = items
        current = value + inverse[None] * following
        return (current, current)

    _, solved = lax.scan(
        backward, jnp.zeros(stacked.shape[1:], jnp.float32), (inverses, values), reverse=True
    )
    return solved


def body(pressure, vel_y, vel_z, material, absorb_table):
    absorb = jnp.zeros(pressure.shape, jnp.float32)
    for entry in range(MATS):
        absorb = absorb + jnp.where(material == entry, absorb_table[entry], 0.0)
    damping = 1.0 / (1.0 + absorb)
    above = passed_along(pressure[:, :1, :], "gy", -1)
    upper_y = jnp.concatenate([pressure[:, 1:, :], above], axis=1)
    upper_z = jnp.concatenate([pressure[:, :, 1:], jnp.zeros_like(pressure[:, :, :1])], axis=2)
    vel_y_next = damping * (vel_y - 0.5 * (upper_y - pressure))
    vel_z_next = damping * (vel_z - 0.5 * (upper_z - pressure))
    below = passed_along(vel_y_next[:, -1:, :], "gy", 1)
    lower_y = jnp.concatenate([below, vel_y_next[:, :-1, :]], axis=1)
    lower_z = jnp.concatenate([jnp.zeros_like(pressure[:, :, :1]), vel_z_next[:, :, :-1]], axis=2)
    source = pressure - 0.5 * (vel_y_next - lower_y + vel_z_next - lower_z)
    line_cells = pressure.shape[0] * lax.axis_size("gx")
    coupling = 1.0 * (line_cells * line_cells // 4)
    excess = (1.0 + absorb) / coupling
    scaled = source / coupling
    rows = lax.broadcasted_iota(jnp.int32, pressure.shape, 0)
    first_unit = jnp.where(rows == 0, -1.0, 0.0)
    last_unit = jnp.where(rows == pressure.shape[0] - 1, -1.0, 0.0)
    stacked = jnp.stack([scaled, first_unit, last_unit], axis=1)
    solved = sweep_lines(excess, stacked)
    local_part = solved[:, 0]
    left_spike = solved[:, 1]
    right_spike = solved[:, 2]
    own = (
        local_part[0],
        -left_spike[0],
        -right_spike[0],
        local_part[-1],
        -left_spike[-1],
        -right_spike[-1],
    )
    nothing = jnp.zeros(local_part.shape[1:], jnp.float32)
    single = jnp.ones(local_part.shape[1:], jnp.float32)
    identity = (nothing, nothing, single, nothing, single, nothing)
    table = (
        lax.all_gather(own[0][None], "gx", axis=0, tiled=True),
        lax.all_gather(own[1][None], "gx", axis=0, tiled=True),
        lax.all_gather(own[2][None], "gx", axis=0, tiled=True),
        lax.all_gather(own[3][None], "gx", axis=0, tiled=True),
        lax.all_gather(own[4][None], "gx", axis=0, tiled=True),
        lax.all_gather(own[5][None], "gx", axis=0, tiled=True),
    )
    position = lax.axis_index("gx")
    indices = jnp.arange(lax.axis_size("gx"), dtype=jnp.int32)

    def take_lower(carry, items):
        index, pieces = items
        merged = join_segments(carry, pieces)
        keep = index < position
        return (tuple((jnp.where(keep, fresh, older) for fresh, older in zip(merged, carry))), None)

    def take_higher(carry, items):
        index, pieces = items
        merged = join_segments(pieces, carry)
        keep = index > position
        return (tuple((jnp.where(keep, fresh, older) for fresh, older in zip(merged, carry))), None)

    prefix, _ = lax.scan(take_lower, identity, (indices, table))
    suffix, _ = lax.scan(take_higher, identity, (indices, table), reverse=True)
    top_rhs = own[0] + own[1] * prefix[3] + own[2] * suffix[0]
    bottom_rhs = own[3] + own[4] * prefix[3] + own[5] * suffix[0]
    top_top = 1.0 - own[1] * prefix[5]
    top_bottom = -own[2] * suffix[1]
    bottom_top = -own[4] * prefix[5]
    bottom_bottom = 1.0 - own[5] * suffix[1]
    determinant = top_top * bottom_bottom - top_bottom * bottom_top
    top_value = (top_rhs * bottom_bottom - top_bottom * bottom_rhs) / determinant
    bottom_value = (top_top * bottom_rhs - bottom_top * top_rhs) / determinant
    before_value = prefix[3] + prefix[5] * top_value
    after_value = suffix[0] + suffix[1] * bottom_value
    pressure_next = local_part - left_spike * before_value[None] - right_spike * after_value[None]
    return (pressure_next, vel_y_next, vel_z_next)


def solution(mesh):
    return jax.shard_map(
        body,
        mesh=mesh,
        in_specs=(
            P("gx", "gy", None),
            P("gx", "gy", None),
            P("gx", "gy", None),
            P("gx", "gy", None),
            P(),
        ),
        out_specs=(P("gx", "gy", None), P("gx", "gy", None), P("gx", "gy", None)),
        check_vma=False,
    )
```

profile of v0, /device:TPU:1, one launch (start us, length us, event | category | flops | bytes accessed | tf_op | source)
XLA Modules:
  0.0 848.9 jit_solution(11246831425350953470)
XLA Ops:
  8.1 1.3 collective-permute-start
  9.4 1.6 fusion.49
  11.0 1.1 slice.93
  12.1 1.2 slice.97
  13.4 6.4 fusion.32
  19.8 4.6 collective-permute-start.1
  25.8 1.4 broadcast.68.clone
  27.2 20.3 %while.64 = (s32[]{:T(128)}, f32[128,128]{1,0:T(8,128)S(1)}, f32[3,128,128]{2,1,0:T(8,128)S(1)}, f32[8,128,128]{2,1,0:T(8,128)S(1)}, f32[8,3,128,128]{3,2,1,0:T(...) while((s32[]{:T(128)}, f32[128,128]{1,0:T(8,128)S(1)}, ...), condition=%wide.region_1.2_spmd.clone, body=%wide.region_0.1_spmd.clone.sunk | while | flops 262147 | bytes 1376881 | solution.py:44
  48.5 15.2 %while.65 = (s32[]{:T(128)}, f32[3,128,128]{2,1,0:T(8,128)S(1)}, f32[8,3,128,128]{3,2,1,0:T(8,128)S(1)}, f32[8,3,128,128]{3,2,1,0:T(8,128)}, f32[8,128,128]{2,1,0:T(8,128)}, /*index=5*/s32[]{:T(128)}, s32[]{:T(128)}, s32[]{:T(128)}) while((s32[]{:T(128)}, f32[3,128,128]{2,1,0:T(8,128)S(1)}, f32[8,3,128,128]{3,2,1,0:T(8,128)S(1)}, ...), condition=%wide.region_3.4_spmd.clone, body=%wide.region_2.3_spmd.clone.sunk | while | flops 147460 | bytes 983155 | solution.py:51
  67.7 81.3 %all-gather.13.cloned.1.call-done = f32[64,1,128,128]{3,2,1,0:T(8,128)} async-done(((f32[1,1,128,128]{3,2,1,0:T(8,128)}), f32[64,1,128,128]{3,2,1,0:T(8,128)}) %all-gather.13.cloned.1.call-update) | async-done | bytes 4194320 | tf_op jit(solution)/shard_map/all_gather | solution.py:98
  149.1 79.5 %all-gather.15.cloned.1.call-done = f32[64,1,128,128]{3,2,1,0:T(8,128)} async-done(((f32[1,1,128,128]{3,2,1,0:T(8,128)}), f32[64,1,128,128]{3,2,1,0:T(8,128)}) %all-gather.15.cloned.1.call-update) | async-done | bytes 4194320 | tf_op jit(solution)/shard_map/all_gather | solution.py:99
  228.6 79.0 %all-gather.17.cloned.1.call-done = f32[64,1,128,128]{3,2,1,0:T(8,128)} async-done(((f32[1,1,128,128]{3,2,1,0:T(8,128)}), f32[64,1,128,128]{3,2,1,0:T(8,128)}) %all-gather.17.cloned.1.call-update) | async-done | bytes 4194320 | tf_op jit(solution)/shard_map/all_gather | solution.py:95
  307.6 78.8 %all-gather.19.cloned.1.call-done = f32[64,1,128,128]{3,2,1,0:T(8,128)} async-done(((f32[1,1,128,128]{3,2,1,0:T(8,128)}), f32[64,1,128,128]{3,2,1,0:T(8,128)}) %all-gather.19.cloned.1.call-update) | async-done | bytes 4194320 | tf_op jit(solution)/shard_map/all_gather | solution.py:96
  386.4 78.8 %all-gather.21.cloned.1.call-done = f32[64,1,128,128]{3,2,1,0:T(8,128)} async-done(((f32[1,1,128,128]{3,2,1,0:T(8,128)}), f32[64,1,128,128]{3,2,1,0:T(8,128)}) %all-gather.21.cloned.1.call-update) | async-done | bytes 4194320 | tf_op jit(solution)/shard_map/all_gather | solution.py:100
  465.2 78.8 %all-gather.23.cloned.1.call-done = f32[64,1,128,128]{3,2,1,0:T(8,128)} async-done(((f32[1,1,128,128]{3,2,1,0:T(8,128)}), f32[64,1,128,128]{3,2,1,0:T(8,128)}) %all-gather.23.cloned.1.call-update) | async-done | bytes 4194320 | tf_op jit(solution)/shard_map/all_gather | solution.py:97
  544.0 148.7 %while.67 = (s32[]{:T(128)}, f32[128,128]{1,0:T(8,128)S(1)}, f32[128,128]{1,0:T(8,128)S(1)}, s32[64]{0:T(128)S(1)}, s32[]{:T(128)}, /*index=5*/f32[64,128,128]{2...) while((s32[]{:T(128)}, f32[128,128]{1,0:T(8,128)S(1)}, ...), condition=%wide.region_7.8_spmd.clone, body=%wide.region_6.7_spmd.clone.sunk | while | flops 278533 | bytes 655541 | solution.py:118
  545.3 1.1 fusion.56
  547.6 1.1 fusion.56
  549.9 1.1 fusion.56
  552.3 1.1 fusion.56
  554.6 1.1 fusion.56
  556.9 1.1 fusion.56
  559.2 1.1 fusion.56
  561.5 1.1 fusion.56
  563.9 1.1 fusion.56
  566.2 1.1 fusion.56
  568.5 1.1 fusion.56
  570.8 1.1 fusion.56
  573.2 1.1 fusion.56
  575.5 1.1 fusion.56
  577.8 1.1 fusion.56
  580.1 1.1 fusion.56
  582.5 1.1 fusion.56
  584.8 1.1 fusion.56
  587.1 1.1 fusion.56
  589.4 1.1 fusion.56
  591.7 1.1 fusion.56
  594.1 1.1 fusion.56
  596.4 1.1 fusion.56
  598.7 1.1 fusion.56
  601.0 1.1 fusion.56
  603.4 1.1 fusion.56
  605.7 1.1 fusion.56
  608.0 1.1 fusion.56
  610.3 1.1 fusion.56
  612.7 1.1 fusion.56
  615.0 1.1 fusion.56
  617.3 1.1 fusion.56
  619.6 1.1 fusion.56
  621.9 1.1 fusion.56
  624.3 1.1 fusion.56
  626.6 1.1 fusion.56
  628.9 1.1 fusion.56
  631.2 1.1 fusion.56
  633.6 1.1 fusion.56
  635.9 1.1 fusion.56
  638.2 1.1 fusion.56
  640.5 1.1 fusion.56
  642.9 1.1 fusion.56
  645.2 1.1 fusion.56
  647.5 1.1 fusion.56
  649.8 1.1 fusion.56
  652.1 1.1 fusion.56
  692.7 148.3 %while.66 = (s32[]{:T(128)}, f32[128,128]{1,0:T(8,128)S(1)}, f32[128,128]{1,0:T(8,128)S(1)}, s32[64]{0:T(128)S(1)}, s32[]{:T(128)}, /*index=5*/f32[64,128,128]{2...) while((s32[]{:T(128)}, f32[128,128]{1,0:T(8,128)S(1)}, ...), condition=%wide.region_5.6_spmd.clone, body=%wide.region_4.5_spmd.clone.sunk | while | flops 245764 | bytes 655521 | solution.py:117
  (299 shorter events, 204.0 us)
Async XLA Ops:
  7.2 6.2 copy-start
  7.2 6.2 copy-start.4
  7.2 6.2 copy-start.5
  7.2 141.9 %all-gather.13.cloned.1.call-start = ((), (), s32[]{:S(2)}) async-start(), calls=%async_computation | async-start | bytes 4259840 | tf_op jit(solution)/shard_map/all_gather | solution.py:98
  7.2 6.2 copy-start.6
  8.1 5.2 collective-permute-start
  19.8 5.7 copy-start.1
  19.8 5.7 copy-start.2
  19.8 5.4 collective-permute-start.1
  47.5 0.8 copy-start.3
  64.5 164.2 %all-gather.15.cloned.1.call-start = ((), (), s32[]{:S(2)}) async-start(), calls=%async_computation.1 | async-start | bytes 4259840 | tf_op jit(solution)/shard_map/all_gather | solution.py:99
  65.2 242.4 %all-gather.17.cloned.1.call-start = ((), (), s32[]{:S(2)}) async-start(), calls=%async_computation.2 | async-start | bytes 4259840 | tf_op jit(solution)/shard_map/all_gather | solution.py:95
  65.9 320.5 %all-gather.19.cloned.1.call-start = ((), (), s32[]{:S(2)}) async-start(), calls=%async_computation.3 | async-start | bytes 4259840 | tf_op jit(solution)/shard_map/all_gather | solution.py:96
  66.5 398.7 %all-gather.21.cloned.1.call-start = ((), (), s32[]{:S(2)}) async-start(), calls=%async_computation.4 | async-start | bytes 4259840 | tf_op jit(solution)/shard_map/all_gather | solution.py:100
  67.1 476.9 %all-gather.23.cloned.1.call-start = ((), (), s32[]{:S(2)}) async-start(), calls=%async_computation.5 | async-start | bytes 4259840 | tf_op jit(solution)/shard_map/all_gather | solution.py:97
Sparse Core Ops, SparseCore 0:
  64.6 84.4 all-gather.12
  152.4 76.1 all-gather.14
  231.4 76.1 all-gather.16
  310.2 76.1 all-gather.18
  389.0 76.1 all-gather.20
  467.8 76.1 all-gather.22
where the time goes:
time: 859 us; the launch traced here: 849 us
  waiting for transfers between devices  480 us (56%)
  other arithmetic  172 us (20%)
  local copies, waits for them, and re-layouts  89.3 us (10%)
  loops' own time  86.8 us (10%)
  between operations  14.4 us (2%)
    all_gather x1, waiting for transfers between devices, body(): lax.all_gather(own[3][None], 'gx', axis=0, tiled=True)  81.3 us
    all_gather x1, waiting for transfers between devices, body(): lax.all_gather(own[4][None], 'gx', axis=0, tiled=True)  79.5 us
    all_gather x1, waiting for transfers between devices, body(): lax.all_gather(own[0][None], 'gx', axis=0, tiled=True)  79 us
    all_gather x1, waiting for transfers between devices, body(): lax.all_gather(own[2][None], 'gx', axis=0, tiled=True)  78.8 us
    all_gather x1, waiting for transfers between devices, body(): lax.all_gather(own[1][None], 'gx', axis=0, tiled=True)  78.8 us
    all_gather x1, waiting for transfers between devices, body(): lax.all_gather(own[5][None], 'gx', axis=0, tiled=True)  78.8 us
    dynamic_slice x128, local copies, waits for them, and re-layouts, body(): prefix, _ = lax.scan(take_lower, identity, (indices, table))  75.1 us
    select_n x64, other arithmetic, take_higher(): jnp.where(keep, fresh, older)  67.8 us
  transfers between devices with their start and end apart: 8, of which 7 were waited for; matrix products, arithmetic and copies ran while one was open for 0% of the time, Pallas kernels for 0%

commit v1 on v0

--- a/solution.py
+++ b/solution.py
@@ -4,6 +4,11 @@
 from jax.sharding import PartitionSpec as P
 
 MATS = 8
+
+
+def tiled_gather(array, axis, dim):
+    copies = jnp.concatenate([array] * lax.axis_size(axis), axis=dim)
+    return lax.all_to_all(copies, axis, dim, dim, tiled=True)
 
 
 def passed_along(value, axis, steps):
@@ -94,7 +99,7 @@
     table = (
         lax.all_gather(own[0][None], "gx", axis=0, tiled=True),
         lax.all_gather(own[1][None], "gx", axis=0, tiled=True),
-        lax.all_gather(own[2][None], "gx", axis=0, tiled=True),
+        tiled_gather(own[2][None], "gx", 0),
         lax.all_gather(own[3][None], "gx", axis=0, tiled=True),
         lax.all_gather(own[4][None], "gx", axis=0, tiled=True),
         lax.all_gather(own[5][None], "gx", axis=0, tiled=True),

time: 859 us -> 801 us (0.932)
  waiting for transfers between devices: 480 us -> 406 us
  starting transfers between devices: 6.16 us -> 19.8 us
    all_to_all x0 -> x1, waiting for transfers between devices: none -> 106 us  [tiled_gather(): return lax.all_to_all(copies, axis, dim, dim, tiled=True)]
    all_gather x1, waiting for transfers between devices: 81.3 us -> 0.01 us  [body(): lax.all_gather(own[3][None], 'gx', axis=0, tiled=True)]
    all_gather x1 -> x0, waiting for transfers between devices: 78.8 us -> none  [body(): lax.all_gather(own[2][None], 'gx', axis=0, tiled=True)]
    all_gather x1, waiting for transfers between devices: 79.5 us -> 60.7 us  [body(): lax.all_gather(own[4][None], 'gx', axis=0, tiled=True)]
    all_to_all x0 -> x1, starting transfers between devices: none -> 13.6 us  [tiled_gather(): return lax.all_to_all(copies, axis, dim, dim, tiled=True)]
  transfers between devices with their start and end apart: 8 -> 8, of which waited for: 7 -> 6; matrix products, arithmetic and copies ran while one was open for 0% -> 1% of each run, Pallas kernels for 0% -> 0%
where the time goes in v1:
time: 801 us; the launch traced here: 791 us
  waiting for transfers between devices  406 us (51%)
  other arithmetic  172 us (21%)
  local copies, waits for them, and re-layouts  91.8 us (11%)
  loops' own time  86.8 us (11%)
  starting transfers between devices  19.8 us (2%)
  between operations  14.1 us (2%)
    all_to_all x1, waiting for transfers between devices, tiled_gather(): return lax.all_to_all(copies, axis, dim, dim, tiled=True)  106 us
    all_gather x1, waiting for transfers between devices, body(): lax.all_gather(own[0][None], 'gx', axis=0, tiled=True)  79 us
    all_gather x1, waiting for transfers between devices, body(): lax.all_gather(own[1][None], 'gx', axis=0, tiled=True)  78.8 us
    all_gather x1, waiting for transfers between devices, body(): lax.all_gather(own[5][None], 'gx', axis=0, tiled=True)  78.8 us
    dynamic_slice x128, local copies, waits for them, and re-layouts, body(): prefix, _ = lax.scan(take_lower, identity, (indices, table))  75.1 us
    select_n x64, other arithmetic, take_higher(): jnp.where(keep, fresh, older)  67.8 us
    select_n x64, other arithmetic, take_lower(): jnp.where(keep, fresh, older)  67.6 us
    all_gather x1, waiting for transfers between devices, body(): lax.all_gather(own[4][None], 'gx', axis=0, tiled=True)  60.7 us
  transfers between devices with their start and end apart: 8, of which 6 were waited for; matrix products, arithmetic and copies ran while one was open for 1% of the time, Pallas kernels for 0%

profile of v1, /device:TPU:1, one launch (start us, length us, event | category | flops | bytes accessed | tf_op | source)
XLA Modules:
  0.0 791.1 jit_solution(14464908604656002919)
XLA Ops:
  8.1 1.3 collective-permute-start
  9.4 1.6 fusion.48
  11.0 1.1 slice.93
  12.1 1.2 slice.97
  13.4 6.3 fusion.32
  19.8 4.6 collective-permute-start.1
  25.8 1.4 broadcast.69.clone
  27.2 20.3 %while.64 = (s32[]{:T(128)}, f32[128,128]{1,0:T(8,128)S(1)}, f32[3,128,128]{2,1,0:T(8,128)S(1)}, f32[8,128,128]{2,1,0:T(8,128)S(1)}, f32[8,3,128,128]{3,2,1,0:T(...) while((s32[]{:T(128)}, f32[128,128]{1,0:T(8,128)S(1)}, ...), condition=%wide.region_1.2_spmd.clone, body=%wide.region_0.1_spmd.clone.sunk | while | flops 262147 | bytes 1376881 | solution.py:49
  48.5 15.2 %while.65 = (s32[]{:T(128)}, f32[3,128,128]{2,1,0:T(8,128)S(1)}, f32[8,3,128,128]{3,2,1,0:T(8,128)S(1)}, f32[8,3,128,128]{3,2,1,0:T(8,128)}, f32[8,128,128]{2,1,0:T(8,128)}, /*index=5*/s32[]{:T(128)}, s32[]{:T(128)}, s32[]{:T(128)}) while((s32[]{:T(128)}, f32[3,128,128]{2,1,0:T(8,128)S(1)}, f32[8,3,128,128]{3,2,1,0:T(8,128)S(1)}, ...), condition=%wide.region_3.4_spmd.clone, body=%wide.region_2.3_spmd.clone.sunk | while | flops 147460 | bytes 983155 | solution.py:56
  66.5 2.5 concatenate.19
  69.0 13.6 %all-to-all-start = ((f32[64,128,128]{2,1,0:T(8,128)}), f32[64,128,128]{2,1,0:T(8,128)}, u32[]{:S(2)}, u32[]{:S(2)}) async-start(f32[64,128,128]{2,1,0:T(8,128)} %concatenate.19), calls=%async_computation | async-start | bytes 8388608 | tf_op jit(solution)/shard_map/all_to_all | solution.py:11
  83.3 105.9 %all-to-all-done = f32[64,128,128]{2,1,0:T(8,128)} async-done(((f32[64,128,128]{2,1,0:T(8,128)}), f32[64,128,128]{2,1,0:T(8,128)}, u32[]{:S(2)}, u32[]{:S(2)}) %all-to-all-start) | async-done | bytes 4194336 | tf_op jit(solution)/shard_map/all_to_all | solution.py:11
  189.2 60.7 %all-gather.13.cloned.1.call-done = f32[64,1,128,128]{3,2,1,0:T(8,128)} async-done(((f32[1,1,128,128]{3,2,1,0:T(8,128)}), f32[64,1,128,128]{3,2,1,0:T(8,128)}) %all-gather.13.cloned.1.call-update) | async-done | bytes 4194320 | tf_op jit(solution)/shard_map/all_gather | solution.py:104
  249.9 79.0 %all-gather.15.cloned.1.call-done = f32[64,1,128,128]{3,2,1,0:T(8,128)} async-done(((f32[1,1,128,128]{3,2,1,0:T(8,128)}), f32[64,1,128,128]{3,2,1,0:T(8,128)}) %all-gather.15.cloned.1.call-update) | async-done | bytes 4194320 | tf_op jit(solution)/shard_map/all_gather | solution.py:100
  328.9 78.8 %all-gather.17.cloned.1.call-done = f32[64,1,128,128]{3,2,1,0:T(8,128)} async-done(((f32[1,1,128,128]{3,2,1,0:T(8,128)}), f32[64,1,128,128]{3,2,1,0:T(8,128)}) %all-gather.17.cloned.1.call-update) | async-done | bytes 4194320 | tf_op jit(solution)/shard_map/all_gather | solution.py:101
  407.7 78.8 %all-gather.19.cloned.1.call-done = f32[64,1,128,128]{3,2,1,0:T(8,128)} async-done(((f32[1,1,128,128]{3,2,1,0:T(8,128)}), f32[64,1,128,128]{3,2,1,0:T(8,128)}) %all-gather.19.cloned.1.call-update) | async-done | bytes 4194320 | tf_op jit(solution)/shard_map/all_gather | solution.py:105
  486.5 148.7 %while.67 = (s32[]{:T(128)}, f32[128,128]{1,0:T(8,128)S(1)}, f32[128,128]{1,0:T(8,128)S(1)}, s32[64]{0:T(128)S(1)}, s32[]{:T(128)}, /*index=5*/f32[64,128,128]{2...) while((s32[]{:T(128)}, f32[128,128]{1,0:T(8,128)S(1)}, ...), condition=%wide.region_7.8_spmd.clone, body=%wide.region_6.7_spmd.clone.sunk | while | flops 278533 | bytes 655541 | solution.py:123
  487.8 1.1 fusion.55
  490.1 1.1 fusion.55
  492.4 1.1 fusion.55
  494.7 1.1 fusion.55
  497.1 1.1 fusion.55
  499.4 1.1 fusion.55
  501.7 1.1 fusion.55
  504.0 1.1 fusion.55
  506.3 1.1 fusion.55
  508.7 1.1 fusion.55
  511.0 1.1 fusion.55
  513.3 1.1 fusion.55
  515.6 1.1 fusion.55
  518.0 1.1 fusion.55
  520.3 1.1 fusion.55
  522.6 1.1 fusion.55
  524.9 1.1 fusion.55
  527.3 1.1 fusion.55
  529.6 1.1 fusion.55
  531.9 1.1 fusion.55
  534.2 1.1 fusion.55
  536.5 1.1 fusion.55
  538.9 1.1 fusion.55
  541.2 1.1 fusion.55
  543.5 1.1 fusion.55
  545.8 1.1 fusion.55
  548.2 1.1 fusion.55
  550.5 1.1 fusion.55
  552.8 1.1 fusion.55
  555.1 1.1 fusion.55
  557.5 1.1 fusion.55
  559.8 1.1 fusion.55
  562.1 1.1 fusion.55
  564.4 1.1 fusion.55
  566.7 1.1 fusion.55
  569.1 1.1 fusion.55
  571.4 1.1 fusion.55
  573.7 1.1 fusion.55
  576.0 1.1 fusion.55
  578.4 1.1 fusion.55
  580.7 1.1 fusion.55
  583.0 1.1 fusion.55
  585.3 1.1 fusion.55
  587.7 1.1 fusion.55
  590.0 1.1 fusion.55
  592.3 1.1 fusion.55
  635.2 148.3 %while.66 = (s32[]{:T(128)}, f32[128,128]{1,0:T(8,128)S(1)}, f32[128,128]{1,0:T(8,128)S(1)}, s32[64]{0:T(128)S(1)}, s32[]{:T(128)}, /*index=5*/f32[64,128,128]{2...) while((s32[]{:T(128)}, f32[128,128]{1,0:T(8,128)S(1)}, ...), condition=%wide.region_5.6_spmd.clone, body=%wide.region_4.5_spmd.clone.sunk | while | flops 245764 | bytes 655521 | solution.py:122
  (300 shorter events, 204.6 us)
Async XLA Ops:
  7.2 6.2 copy-start
  7.2 6.2 copy-start.4
  7.2 6.2 copy-start.5
  7.2 182.0 %all-gather.11.cloned.1.call-start = ((), (), s32[]{:S(2)}) async-start(), calls=%async_computation.1 | async-start | bytes 4259840 | tf_op jit(solution)/shard_map/all_gather | solution.py:103
  7.2 6.2 copy-start.6
  8.1 5.2 collective-permute-start
  19.8 5.7 copy-start.1
  19.8 5.7 copy-start.2
  19.8 5.4 collective-permute-start.1
  47.5 0.8 copy-start.3
  64.5 185.5 %all-gather.13.cloned.1.call-start = ((), (), s32[]{:S(2)}) async-start(), calls=%async_computation.2 | async-start | bytes 4259840 | tf_op jit(solution)/shard_map/all_gather | solution.py:104
  65.2 263.7 %all-gather.15.cloned.1.call-start = ((), (), s32[]{:S(2)}) async-start(), calls=%async_computation.3 | async-start | bytes 4259840 | tf_op jit(solution)/shard_map/all_gather | solution.py:100
  65.9 341.8 %all-gather.17.cloned.1.call-start = ((), (), s32[]{:S(2)}) async-start(), calls=%async_computation.4 | async-start | bytes 4259840 | tf_op jit(solution)/shard_map/all_gather | solution.py:101
  69.0 120.2 %all-to-all-start = ((f32[64,128,128]{2,1,0:T(8,128)}), f32[64,128,128]{2,1,0:T(8,128)}, u32[]{:S(2)}, u32[]{:S(2)}) async-start(f32[64,128,128]{2,1,0:T(8,128)} %concatenate.19), calls=%async_computation | async-start | bytes 8388608 | tf_op jit(solution)/shard_map/all_to_all | solution.py:11
  82.7 403.8 %all-gather.19.cloned.1.call-start = ((), (), s32[]{:S(2)}) async-start(), calls=%async_computation.5 | async-start | bytes 4259840 | tf_op jit(solution)/shard_map/all_gather | solution.py:105
Sparse Core Ops, SparseCore 0:
  64.6 103.2 all-gather.10
  171.2 78.6 all-gather.12
  252.7 76.1 all-gather.14
  331.5 76.1 all-gather.16
  410.3 76.1 all-gather.18
